TPU v7x, 128 devices: a whole 4x4x4 slice. The times are simulated.
128 devices in a mesh: seq: 16 (over x, z), guid: 2 (over core), tp: 4 (over y).
Axes of the slice: x: 4, y: 4, z: 4, core: 2. Of those that a mesh axis runs over, the one named last changes fastest.
Arguments:
- hidden_states: bfloat16 [2, 6144, 3072], P('guid', 'seq'), may hold values from -6 to 6
- modulation: float32 [2, 3, 3072], P('guid')
- w_query: bfloat16 [3072, 3072], P(None, 'tp'), may hold values from -0.109375 to 0.109375
- w_key: bfloat16 [3072, 3072], P(None, 'tp'), may hold values from -0.109375 to 0.109375
- w_value: bfloat16 [3072, 3072], P(None, 'tp'), may hold values from -0.109375 to 0.109375
- w_out: bfloat16 [3072, 3072], P('tp'), may hold values from -0.109375 to 0.109375
- block_ids: int32 [48, 12], P('seq'), may hold values from 0 to 47, as said below
- block_count: int32 [48], P('seq'), may hold values from 1 to 12, as said below
- guidance: float32 [1], replicated, may hold values from 4 to 8
Outputs:
- guided: bfloat16 [6144, 3072], P('seq', ('guid', 'tp'))
Inputs may be any that keep to these rules, and one draw needn't show every extreme that they name: `block_ids`: entry 0 of each list is the query tile itself; the first block_count entries are distinct tiles within 12 tiles of the query tile; later entries repeat the query tile. `block_count`: some query tile lists 12 tiles.
All inputs are finite; a program needn't handle non-finite values.
Results may differ from a plain program's by a relative error of at most 0.02.
The roundings to bfloat16 on the way count: a program that leaves them out, or rounds other values in their place, can miss the bound.
Values may be sent and summed in bfloat16 or wider, within the bound.
A program may use at most 192 MiB of HBM per device.

v0:
```python
import functools
import math

import jax
import jax.numpy as jnp
from jax import lax
from jax.experimental import pallas as pl
from jax.experimental.pallas import tpu as pltpu
from jax.sharding import PartitionSpec as P

HD = 64
TILE = 128
MESH = pl.DeviceIdType.MESH
EXP_SCALE = 0.125 * math.log2(math.e)

NZ = 4
OWN_TILES = 3
SLAB = NZ * OWN_TILES
ROUNDS = 3
SLOTS = 12
TOK = OWN_TILES * TILE
GROUP = NZ * HD


def attention_kernel(
    x_hbm,
    mod_ref,
    wq_hbm,
    wk_hbm,
    wv_hbm,
    ids_ref,
    count_ref,
    out_ref,
    xbuf,
    hbuf,
    wbuf,
    stage,
    kv_0,
    kv_1,
    kv_2,
    qstage,
    qbuf,
    ret,
    back,
    scores,
    meta,
    meta_all,
    meta_smem,
    load_sem,
    z_send,
    z_recv,
    x_send,
    x_recv,
    q_send,
    q_recv,
    r_send,
    r_recv,
    m_send,
    m_recv,
    local_sem,
):
    seq = lax.axis_index("seq")
    guid = lax.axis_index("guid")
    tp = lax.axis_index("tp")
    px = seq // NZ
    pz = seq % NZ
    kv = (kv_0, kv_1, kv_2)

    def z_peer(dz):
        return (px * NZ + (pz + dz) % NZ, guid, tp)

    def x_peer(dx):
        return (((px + dx + NZ) % NZ) * NZ + pz, guid, tp)

    x_copy = pltpu.make_async_copy(x_hbm, xbuf, load_sem.at[9])
    x_copy.start()
    weights = {}
    order = [(kind, j) for j in range(ROUNDS) for kind in (1, 2)] + [(0, j) for j in range(ROUNDS)]
    for kind, j in order:
        source = (wq_hbm, wk_hbm, wv_hbm)[kind]
        slot = kind * ROUNDS + j
        copy = pltpu.make_async_copy(
            source.at[:, pl.ds(j * GROUP, GROUP)], wbuf.at[slot], load_sem.at[slot]
        )
        copy.start()
        weights[slot] = copy

    meta[...] = jnp.zeros_like(meta)
    meta[0:3, 0:SLOTS] = ids_ref[...]
    meta[3:4, 0:3] = count_ref[...]
    meta_all[pz] = meta[...]

    barrier = pltpu.get_barrier_semaphore()
    peers = [z_peer(dz) for dz in (1, 2, 3)] + [x_peer(dx) for dx in (1, -1)]
    for peer in peers:
        pl.semaphore_signal(barrier, inc=1, device_id=peer, device_id_type=MESH)
    pl.semaphore_wait(barrier, len(peers))

    def meta_copy(dz):
        return pltpu.make_async_remote_copy(
            src_ref=meta,
            dst_ref=meta_all.at[pz],
            send_sem=m_send.at[dz - 1],
            recv_sem=m_recv.at[dz - 1],
            device_id=z_peer(dz),
            device_id_type=MESH,
        )

    def z_copy(j, dz):
        return pltpu.make_async_remote_copy(
            src_ref=stage.at[j, (pz + dz) % NZ],
            dst_ref=kv[j].at[pl.ds(SLAB + pz * OWN_TILES, OWN_TILES)],
            send_sem=z_send.at[j, dz - 1],
            recv_sem=z_recv.at[j, dz - 1],
            device_id=z_peer(dz),
            device_id_type=MESH,
        )

    def own_copy(j):
        return pltpu.make_async_copy(
            stage.at[j, pz],
            kv[j].at[pl.ds(SLAB + pz * OWN_TILES, OWN_TILES)],
            local_sem.at[j],
        )

    def x_copy_of(j, dz, side):
        origin = (pz - dz + NZ) % NZ
        here = kv[j].at[pl.ds(SLAB + origin * OWN_TILES, OWN_TILES)]
        return pltpu.make_async_remote_copy(
            src_ref=stage.at[j, pz] if dz == 0 else here,
            dst_ref=kv[j].at[pl.ds(2 * SLAB * side + origin * OWN_TILES, OWN_TILES)],
            send_sem=x_send.at[j, dz, side],
            recv_sem=x_recv.at[j, dz, side],
            device_id=x_peer(1 - 2 * side),
            device_id_type=MESH,
        )

    def q_copy(j, dz):
        return pltpu.make_async_remote_copy(
            src_ref=qstage.at[j, (pz + dz) % NZ],
            dst_ref=qbuf.at[j, pz],
            send_sem=q_send.at[j, dz - 1],
            recv_sem=q_recv.at[j, dz - 1],
            device_id=z_peer(dz),
            device_id_type=MESH,
        )

    def r_copy(j, dz):
        return pltpu.make_async_remote_copy(
            src_ref=ret.at[j, (pz + dz) % NZ],
            dst_ref=back.at[j, pz],
            send_sem=r_send.at[j, dz - 1],
            recv_sem=r_recv.at[j, dz - 1],
            device_id=z_peer(dz),
            device_id_type=MESH,
        )

    for dz in (1, 2, 3):
        meta_copy(dz).start()

    x_copy.wait()
    rows = 16

    def norm_rows(i, carry):
        at = pl.ds(pl.multiple_of(i * rows, rows), rows)
        xf = xbuf[at, :].astype(jnp.float32)
        width = xf.shape[1]
        mean = jnp.sum(xf, axis=1, keepdims=True) * (1.0 / width)
        off = xf - mean
        var = jnp.sum(off * off, axis=1, keepdims=True) * (1.0 / width)
        scale = 1.0 / jnp.sqrt(var + 1e-05)
        hbuf[at, :] = (off * scale * (1.0 + mod_ref[1:2, :]) + mod_ref[0:1, :]).astype(
            jnp.bfloat16
        )
        return carry

    lax.fori_loop(0, TOK // rows, norm_rows, 0)

    def product(slot):
        weights[slot].wait()
        full = jnp.dot(hbuf[...], wbuf[slot], preferred_element_type=jnp.float32)
        return full.astype(jnp.bfloat16)

    def tiles_of(full):
        for i in range(OWN_TILES):
            part = full[i * TILE : (i + 1) * TILE, :]
            yield i, jnp.transpose(part).reshape(NZ, HD, TILE)

    def make_kv(j):
        for which in (0, 1):
            for i, part in tiles_of(product((1 + which) * ROUNDS + j)):
                stage[j, :, i, which] = part

    def forward(j):
        for dz in (1, 2, 3):
            z_copy(j, dz).wait_recv()
            for side in (0, 1):
                x_copy_of(j, dz, side).start()

    def make_q(j):
        for i, part in tiles_of(product(j)):
            qstage[j, :, i] = part
        for dz in (1, 2, 3):
            q_copy(j, dz).start()
        qbuf[j, pz] = qstage[j, pz]

    for j in range(ROUNDS):
        make_kv(j)
        for dz in (1, 2, 3):
            z_copy(j, dz).start()
        for side in (0, 1):
            x_copy_of(j, 0, side).start()
        own_copy(j).start()
    forward(0)
    make_q(0)
    forward(1)
    make_q(1)
    forward(2)
    make_q(2)

    for dz in (1, 2, 3):
        meta_copy(dz).wait_recv()
    meta_load = pltpu.make_async_copy(meta_all, meta_smem, local_sem.at[3])
    meta_load.start()
    meta_load.wait()

    first = (px - 1) * SLAB
    one_rows = jnp.ones((HD, TILE), jnp.bfloat16)
    zero_rows = jnp.zeros((HD, TILE), jnp.bfloat16)

    def attend(j, owner, i):
        q = jnp.transpose(qbuf[j, owner, i])
        top = None
        where = []
        for c in range(0, SLOTS, 2):
            spots = [
                jnp.clip(meta_smem[owner, i, c + e] - first, 0, 3 * SLAB - 1) for e in (0, 1)
            ]
            where.append(spots)
            pair = jnp.concatenate([kv[j][spot, 0] for spot in spots], axis=1)
            s = jnp.dot(q, pair, preferred_element_type=jnp.float32)
            scores[i, c // 2] = s
            top = s if top is None else jnp.maximum(top, s)
        top = jnp.max(top, axis=1, keepdims=True)
        live = meta_smem[owner, 3, i]
        acc = None
        for c in range(0, SLOTS, 2):
            p = jnp.exp2((scores[i, c // 2] - top) * EXP_SCALE).astype(jnp.bfloat16)
            sides = []
            for e in (0, 1):
                ok = (c + e) < live
                spot = where[c // 2][e]
                sides.append(
                    jnp.concatenate(
                        [
                            jnp.where(ok, kv[j][spot, 1], zero_rows),
                            jnp.where(ok, one_rows, zero_rows),
                        ],
                        axis=0,
                    )
                )
            values = jnp.concatenate(sides, axis=1)
            part = lax.dot_general(
                p, values, (((1,), (1,)), ((), ())), preferred_element_type=jnp.float32
            )
            acc = part if acc is None else acc + part
        both = jnp.transpose(acc)
        ret[j, owner, i] = (both[:HD] / both[HD:]).astype(jnp.bfloat16)

    for j in range(ROUNDS):
        own_copy(j).wait()
        for dz in (0, 1, 2, 3):
            for side in (0, 1):
                x_copy_of(j, dz, side).wait_recv()
        for dz in (1, 2, 3):
            q_copy(j, dz).wait_recv()

        def owner_step(step, carry, j=j):
            dz = (step + 1) % NZ
            owner = (pz + dz) % NZ
            for i in range(OWN_TILES):
                attend(j, owner, i)

            return carry

        lax.fori_loop(0, NZ, owner_step, 0)
        for dz in (1, 2, 3):
            r_copy(j, dz).start()
        back[j, pz] = ret[j, pz]

    for j in range(ROUNDS):
        for dz in (1, 2, 3):
            r_copy(j, dz).wait_recv()
        for i in range(OWN_TILES):
            part = back[j, :, i].reshape(GROUP, TILE)
            out_ref[pl.ds(i * TILE, TILE), pl.ds(j * GROUP, GROUP)] = jnp.transpose(part)

    for dz in (1, 2, 3):
        meta_copy(dz).wait_send()
    for j in range(ROUNDS):
        for dz in (1, 2, 3):
            z_copy(j, dz).wait_send()
            q_copy(j, dz).wait_send()
            r_copy(j, dz).wait_send()
        for dz in (0, 1, 2, 3):
            for side in (0, 1):
                x_copy_of(j, dz, side).wait_send()


def attention(states, modul, w_query, w_key, w_value, block_ids, block_count):
    width = states.shape[1]
    bf16 = jnp.bfloat16
    dma = pltpu.SemaphoreType.DMA
    any_spec = pl.BlockSpec(memory_space=pltpu.HBM)
    vmem_spec = pl.BlockSpec(memory_space=pltpu.VMEM)
    return pl.pallas_call(
        attention_kernel,
        out_shape=jax.ShapeDtypeStruct((TOK, ROUNDS * GROUP), bf16),
        in_specs=[any_spec, vmem_spec, any_spec, any_spec, any_spec, vmem_spec, vmem_spec],
        out_specs=vmem_spec,
        scratch_shapes=[
            pltpu.VMEM((TOK, width), bf16),
            pltpu.VMEM((TOK, width), bf16),
            pltpu.VMEM((3 * ROUNDS, width, GROUP), bf16),
            pltpu.VMEM((ROUNDS, NZ, OWN_TILES, 2, HD, TILE), bf16),
            pltpu.VMEM((3 * SLAB, 2, HD, TILE), bf16),
            pltpu.VMEM((3 * SLAB, 2, HD, TILE), bf16),
            pltpu.VMEM((3 * SLAB, 2, HD, TILE), bf16),
            pltpu.VMEM((ROUNDS, NZ, OWN_TILES, HD, TILE), bf16),
            pltpu.VMEM((ROUNDS, NZ, OWN_TILES, HD, TILE), bf16),
            pltpu.VMEM((ROUNDS, NZ, OWN_TILES, HD, TILE), bf16),
            pltpu.VMEM((ROUNDS, NZ, OWN_TILES, HD, TILE), bf16),
            pltpu.VMEM((OWN_TILES, SLOTS // 2, TILE, 2 * TILE), jnp.float32),
            pltpu.VMEM((8, 128), jnp.int32),
            pltpu.VMEM((NZ, 8, 128), jnp.int32),
            pltpu.SMEM((NZ, 8, 128), jnp.int32),
            dma((10,)),
            dma((ROUNDS, 3)),
            dma((ROUNDS, 3)),
            dma((ROUNDS, 4, 2)),
            dma((ROUNDS, 4, 2)),
            dma((ROUNDS, 3)),
            dma((ROUNDS, 3)),
            dma((ROUNDS, 3)),
            dma((ROUNDS, 3)),
            dma((3,)),
            dma((3,)),
            dma((4,)),
        ],
        compiler_params=pltpu.CompilerParams(
            collective_id=0, has_side_effects=True, vmem_limit_bytes=56 * 2**20
        ),
        name="attention",
    )(states, modul, w_query, w_key, w_value, block_ids, block_count)


def swapped(value, axis, distance):
    return lax.ppermute(value, axis, [(i, i ^ 1 << distance) for i in range(lax.axis_size(axis))])


def shards(
    hidden_states, modulation, w_query, w_key, w_value, w_out, block_ids, block_count, guidance
):
    states = hidden_states[0]
    modul = modulation[0]
    ntok = states.shape[0]
    attn = attention(
        states, modul, w_query, w_key, w_value, block_ids, block_count.reshape(1, -1)
    )
    xf = states.astype(jnp.float32)
    proj = jnp.dot(attn, w_out, preferred_element_type=jnp.float32)
    scale_now = guidance[0]
    branch = lax.axis_index("guid")
    tp_count = lax.axis_size("tp")
    tp_here = lax.axis_index("tp")
    model_width = states.shape[1]
    half = model_width // (2 * tp_count)

    def regroup(array):
        count = array.shape[0]
        return jnp.transpose(array.reshape(count, 2, tp_count, half), (0, 2, 1, 3)).reshape(
            count, model_width
        )

    shares = lax.psum_scatter(
        regroup(proj).astype(jnp.bfloat16), "tp", scatter_dimension=1, tiled=True
    ).astype(jnp.float32)
    x_part = lax.dynamic_slice_in_dim(regroup(xf), tp_here * 2 * half, 2 * half, 1)
    gate_part = lax.dynamic_slice_in_dim(
        regroup(modul[2][None, :]), tp_here * 2 * half, 2 * half, 1
    )
    block = (x_part + gate_part * shares).reshape(ntok, 2, half)
    own = lax.dynamic_slice_in_dim(block, branch, 1, 1)[:, 0]
    outgoing = lax.dynamic_slice_in_dim(block, 1 - branch, 1, 1)[:, 0]
    other = swapped(outgoing.astype(jnp.bfloat16), "guid", 0).astype(outgoing.dtype)
    cond = jnp.where(branch == 0, own, other)
    uncond = jnp.where(branch == 0, other, own)
    return (uncond + scale_now * (cond - uncond)).astype(jnp.bfloat16)


def solution(mesh):
    in_specs = (
        P("guid", "seq", None),
        P("guid", None, None),
        P(None, "tp"),
        P(None, "tp"),
        P(None, "tp"),
        P("tp", None),
        P("seq", None),
        P("seq"),
        P(),
    )
    out_specs = P("seq", ("guid", "tp"))
    return jax.shard_map(shards, mesh=mesh, in_specs=in_specs, out_specs=out_specs, check_vma=False)
```

profile of v0, /device:TPU:1, one launch (start us, length us, event | category | flops | bytes accessed | tf_op | source)
XLA Modules:
  0.0 120.6 jit_solution(2006510951218451730)
XLA Ops:
  6.5 0.0 reduce-scatter.2.cloned.1.call-start
  6.5 1.4 %copy.21 = f32[1,3,3072]{2,1,0:T(4,128)} copy(f32[1,3,3072]{2,0,1:T(1,128)} %param.10) | data formatting | bytes 73728
  7.9 0.0 copy-start.1
  7.9 55.8 %attention.1 = bf16[384,768]{1,0:T(8,128)(2,1)} custom-call(bf16[384,3072]{1,0:T(8,128)(2,1)} %bitcast.25, f32[3,3072]{1,0:T(4,128)} %bitcast.31, bf16[3072,768]{1,0:T(8,128)(2,1)} %wq_hbm.1, bf16[3072,768]{1,0:T(8,128)(2,1)} %wk_hbm.1, bf16[3072,768]{1,0:T(8,128)(2,1)} %wv_hbm.1, s32[3,12]{1,0:T(4,128)} %ids_ref.1, s32[1,3]{1,0:T(1,128)} %bitcast.33), custom_call_target="tpu_custom_call" | custom-call | tf_op jit(solution)/shard_map/attention/pallas_call | solution.py:316
  63.7 0.0 copy-done.1
  63.7 4.5 %convolution_convert_fusion = bf16[384,3072]{1,0:T(8,128)(2,1)} fusion(bf16[384,768]{1,0:T(8,128)(2,1)} %attention.1, bf16[768,3072]{1,0:T(8,128)(2,1)S(1)} %copy-done.1), kind=kOutput, calls=%fused_computation.1 | convolution fusion | flops 1813118976 | bytes 7667712 | tf_op jit(solution)/shard_map/dot_general | solution.py:371
  68.2 4.5 %convert_element_type.34 = bf16[384,2,4,384]{3,2,1,0:T(4,128)(2,1)S(1)} reshape(bf16[384,3072]{1,0:T(8,128)(2,1)} %convolution_convert_fusion) | data formatting | bytes 4718592 | tf_op jit(solution)/shard_map/convert_element_type | solution.py:386
  72.7 3.7 %copy.16 = bf16[384,2,4,384]{0,3,1,2:T(8,128)(2,1)} copy(bf16[384,2,4,384]{3,2,1,0:T(4,128)(2,1)S(1)} %convert_element_type.34) | data formatting | bytes 4718592 | tf_op jit(solution)/shard_map/convert_element_type | solution.py:386
  76.4 0.0 copy-start
  76.4 0.0 reduce-scatter.2.cloned.1.call-update
  76.4 1.6 %copy-done = bf16[1,384,3072]{2,1,0:T(8,128)(2,1)S(1)} copy-done((bf16[1,384,3072]{2,1,0:T(8,128)(2,1)S(1)}, bf16[1,384,3072]{2,1,0:T(8,128)(2,1)}, u32[]{:S(2)}) %copy-start) | copy-done | bytes 2359320
  78.1 2.4 %copy.13 = bf16[1,384,3072]{1,2,0:T(8,128)(2,1)} copy(bf16[1,384,3072]{2,1,0:T(8,128)(2,1)S(1)} %copy-done) | data formatting | bytes 4718592 | tf_op args[0]
  80.5 0.7 slice_reduce_fusion
  81.3 2.0 %convert_bitcast_fusion = f32[384,4,2,384]{0,3,1,2:T(8,128)S(1)} fusion(bf16[384,2,4,384]{0,3,2,1:T(8,128)(2,1)} %bitcast.26), kind=kLoop, calls=%fused_computation | loop fusion | flops 1179648 | bytes 7077888 | tf_op jit(solution)/shard_map/reshape | solution.py:381
  83.3 2.4 %copy.14 = f32[384,4,2,384]{0,3,2,1:T(8,128)} copy(f32[384,4,2,384]{0,3,1,2:T(8,128)S(1)} %convert_bitcast_fusion) | data formatting | bytes 9437184 | tf_op jit(solution)/shard_map/reshape | solution.py:381
  85.7 23.4 %reduce-scatter.2.cloned.1.call-done = bf16[384,768]{0,1:T(8,128)(2,1)} async-done(((bf16[384,3072]{0,1:T(8,128)(2,1)}), bf16[384,768]{0,1:T(8,128)(2,1)}) %reduce-scatter.2.cloned.1.call-update) | async-done | bytes 589840 | tf_op jit(solution)/shard_map/reduce_scatter | solution.py:385
  109.1 1.7 %multiply_add_fusion = f32[384,768]{0,1:T(8,128)S(1)} fusion(bf16[384,768]{0,1:T(8,128)(2,1)} %reduce-scatter.2.cloned.1.call-done, f32[384,3072]{0,1:T(8,128)} %bitcast.28, s32[]{:T(128)S(6)} %select_n.23, f32[768]{0:T(1024)S(1)} %dynamic-slice_reduce_fusion), kind=kLoop, calls=%fused_computation.2 | loop fusion | flops 884736 | bytes 2952196 | tf_op jit(solution)/shard_map/add | solution.py:392
  110.8 0.7 collective-permute-start
  112.2 0.6 collective-permute-done
  112.7 0.1 fusion.3
  112.9 0.9 copy.17
  (5 shorter events, 0.1 us)
Async XLA Ops:
  6.5 102.6 %reduce-scatter.2.cloned.1.call-start = ((), (), s32[]{:S(2)}) async-start(), calls=%async_computation.1 | async-start | bytes 2949120 | tf_op jit(solution)/shard_map/reduce_scatter | solution.py:385
  7.9 55.8 %copy-start.1 = (bf16[768,3072]{1,0:T(8,128)(2,1)S(1)}, bf16[768,3072]{1,0:T(8,128)(2,1)}, u32[]{:S(2)}) copy-start(bf16[768,3072]{1,0:T(8,128)(2,1)} %param.14) | copy-start | bytes 14155780
  76.4 1.7 %copy-start = (bf16[1,384,3072]{2,1,0:T(8,128)(2,1)S(1)}, bf16[1,384,3072]{2,1,0:T(8,128)(2,1)}, u32[]{:S(2)}) copy-start(bf16[1,384,3072]{2,1,0:T(8,128)(2,1)} %param.9) | copy-start | bytes 7077892
  110.8 1.9 %collective-permute-start = (bf16[384,384]{0,1:T(8,128)(2,1)S(1)}, bf16[384,384]{0,1:T(8,128)(2,1)S(1)}, u32[]{:S(2)}, u32[]{:S(2)}) collective-permute-start(bf16[384,384]{0,1:T(8,128)(2,1)S(1)} %fusion.4), channel_id=1, source_target_pairs={{0,4},{4,0},{1,5},{5,1},{2,6},{6,2},{3,7},{7,3},{8,12},{12,8},{9,1... | collective-permute-start | bytes 884744 | tf_op jit(solution)/shard_map/ppermute | solution.py:358
Sparse Core Ops, SparseCore 0:
  76.5 32.5 reduce-scatter.1
where the time goes:
time: 121 us
  Pallas kernels  55.8 us (46%)
  waiting for transfers between devices  24 us (20%)
  local copies, waits for them, and re-layouts  17.8 us (15%)
  between operations  14.1 us (12%)
  matrix products  4.48 us (4%)
  other arithmetic  3.77 us (3%)
    pallas_call x1, Pallas kernels, attention(): pl.pallas_call(attention_kernel, out_shape=jax.ShapeDtypeStruct((TOK, ROU...  55.8 us
    reduce_scatter x1, waiting for transfers between devices, shards(): lax.psum_scatter(regroup(proj).astype(jnp.bfloat16), 'tp', scatter_dimens...  23.4 us
    convert_element_type x2, local copies, waits for them, and re-layouts, shards(): regroup(proj).astype(jnp.bfloat16)  8.19 us
    unnamed x6, local copies, waits for them, and re-layouts  5.47 us
    dot_general x1, matrix products, shards(): proj = jnp.dot(attn, w_out, preferred_element_type=jnp.float32)  4.48 us
    reshape x2, local copies, waits for them, and re-layouts, regroup(): jnp.transpose(array.reshape(count, 2, tp_count, half), (0, 2, 1, 3))  2.45 us
  transfers between devices with their start and end apart: 2, of which 2 were waited for; matrix products, arithmetic and copies ran while one was open for 6% of the time, Pallas kernels for 0%

commit v1 on v0

--- a/solution.py
+++ b/solution.py
@@ -14,6 +14,7 @@
 EXP_SCALE = 0.125 * math.log2(math.e)
 
 NZ = 4
+NY = 4
 OWN_TILES = 3
 SLAB = NZ * OWN_TILES
 ROUNDS = 3
@@ -22,14 +23,16 @@
 GROUP = NZ * HD
 
 
-def attention_kernel(
+def block_kernel(
     x_hbm,
     mod_ref,
     wq_hbm,
     wk_hbm,
     wv_hbm,
+    wo_hbm,
     ids_ref,
     count_ref,
+    guidance_ref,
     out_ref,
     xbuf,
     hbuf,
@@ -43,6 +46,11 @@
     ret,
     back,
     scores,
+    wo,
+    abuf,
+    acc,
+    xother,
+    modother,
     meta,
     meta_all,
     meta_smem,
@@ -57,6 +65,14 @@
     r_recv,
     m_send,
     m_recv,
+    w_send,
+    w_recv,
+    y_send,
+    y_recv,
+    c_send,
+    c_recv,
+    p_send,
+    p_recv,
     local_sem,
 ):
     seq = lax.axis_index("seq")
@@ -72,7 +88,12 @@
     def x_peer(dx):
         return (((px + dx + NZ) % NZ) * NZ + pz, guid, tp)
 
-    x_copy = pltpu.make_async_copy(x_hbm, xbuf, load_sem.at[9])
+    def y_peer(dy):
+        return (seq, guid, (tp + dy) % NY)
+
+    partner = (seq, 1 - guid, tp)
+
+    x_copy = pltpu.make_async_copy(x_hbm.at[0], xbuf, load_sem.at[9])
     x_copy.start()
     weights = {}
     order = [(kind, j) for j in range(ROUNDS) for kind in (1, 2)] + [(0, j) for j in range(ROUNDS)]
@@ -85,6 +106,13 @@
         copy.start()
         weights[slot] = copy
 
+    wo_own = pltpu.make_async_copy(
+        wo_hbm.at[:, pl.ds(pl.multiple_of((guid * NY + tp) * TOK, TILE), TOK)],
+        wo.at[tp],
+        load_sem.at[10],
+    )
+    wo_own.start()
+
     meta[...] = jnp.zeros_like(meta)
     meta[0:3, 0:SLOTS] = ids_ref[...]
     meta[3:4, 0:3] = count_ref[...]
@@ -92,6 +120,7 @@
 
     barrier = pltpu.get_barrier_semaphore()
     peers = [z_peer(dz) for dz in (1, 2, 3)] + [x_peer(dx) for dx in (1, -1)]
+    peers += [y_peer(dy) for dy in (1, 2, 3)] + [partner]
     for peer in peers:
         pl.semaphore_signal(barrier, inc=1, device_id=peer, device_id_type=MESH)
     pl.semaphore_wait(barrier, len(peers))
@@ -155,10 +184,61 @@
             device_id_type=MESH,
         )
 
+    def w_copy(dy):
+        column = (guid * NY + (tp + dy) % NY) * TOK
+        return pltpu.make_async_remote_copy(
+            src_ref=wo_hbm.at[:, pl.ds(pl.multiple_of(column, TILE), TOK)],
+            dst_ref=wo.at[tp],
+            send_sem=w_send.at[dy - 1],
+            recv_sem=w_recv.at[dy - 1],
+            device_id=y_peer(dy),
+            device_id_type=MESH,
+        )
+
+    def y_copy(j, dy):
+        return pltpu.make_async_remote_copy(
+            src_ref=abuf.at[guid, tp, j],
+            dst_ref=abuf.at[guid, tp, j],
+            send_sem=y_send.at[j, dy - 1],
+            recv_sem=y_recv.at[j, dy - 1],
+            device_id=y_peer(dy),
+            device_id_type=MESH,
+        )
+
+    def c_copy(j, dy):
+        origin = (tp - dy + NY) % NY
+        return pltpu.make_async_remote_copy(
+            src_ref=abuf.at[guid, origin, j],
+            dst_ref=abuf.at[guid, origin, j],
+            send_sem=c_send.at[j, dy],
+            recv_sem=c_recv.at[j, dy],
+            device_id=partner,
+            device_id_type=MESH,
+        )
+
+    def p_copy(which):
+        if which == 0:
+            column = ((1 - guid) * NY + tp) * TOK
+            source, target = xbuf.at[:, pl.ds(pl.multiple_of(column, TILE), TOK)], xother
+        else:
+            source, target = mod_ref, modother
+        return pltpu.make_async_remote_copy(
+            src_ref=source,
+            dst_ref=target,
+            send_sem=p_send.at[which],
+            recv_sem=p_recv.at[which],
+            device_id=partner,
+            device_id_type=MESH,
+        )
+
     for dz in (1, 2, 3):
         meta_copy(dz).start()
+    for dy in (1, 3, 2):
+        w_copy(dy).start()
 
     x_copy.wait()
+    for which in (0, 1):
+        p_copy(which).start()
     rows = 16
 
     def norm_rows(i, carry):
@@ -169,7 +249,7 @@
         off = xf - mean
         var = jnp.sum(off * off, axis=1, keepdims=True) * (1.0 / width)
         scale = 1.0 / jnp.sqrt(var + 1e-05)
-        hbuf[at, :] = (off * scale * (1.0 + mod_ref[1:2, :]) + mod_ref[0:1, :]).astype(
+        hbuf[at, :] = (off * scale * (1.0 + mod_ref[1]) + mod_ref[0]).astype(
             jnp.bfloat16
         )
         return carry
@@ -267,7 +347,7 @@
         both = jnp.transpose(acc)
         ret[j, owner, i] = (both[:HD] / both[HD:]).astype(jnp.bfloat16)
 
-    for j in range(ROUNDS):
+    def attention_round(j):
         own_copy(j).wait()
         for dz in (0, 1, 2, 3):
             for side in (0, 1):
@@ -275,12 +355,10 @@
         for dz in (1, 2, 3):
             q_copy(j, dz).wait_recv()
 
-        def owner_step(step, carry, j=j):
-            dz = (step + 1) % NZ
-            owner = (pz + dz) % NZ
+        def owner_step(step, carry):
+            owner = (pz + step + 1) % NZ
             for i in range(OWN_TILES):
                 attend(j, owner, i)
-
             return carry
 
         lax.fori_loop(0, NZ, owner_step, 0)
@@ -288,16 +366,82 @@
             r_copy(j, dz).start()
         back[j, pz] = ret[j, pz]
 
-    for j in range(ROUNDS):
+    def gather(j):
         for dz in (1, 2, 3):
             r_copy(j, dz).wait_recv()
         for i in range(OWN_TILES):
             part = back[j, :, i].reshape(GROUP, TILE)
-            out_ref[pl.ds(i * TILE, TILE), pl.ds(j * GROUP, GROUP)] = jnp.transpose(part)
-
+            abuf[guid, tp, j, pl.ds(i * TILE, TILE), :] = jnp.transpose(part)
+        for dy in (1, 3, 2):
+            y_copy(j, dy).start()
+        c_copy(j, 0).start()
+
+    def spread(j):
+        for dy in (1, 3, 2):
+            y_copy(j, dy).wait_recv()
+            c_copy(j, dy).start()
+
+    def product_of(branch, js):
+        def one(y, carry):
+            total = None
+            for j in js:
+                part = jnp.dot(
+                    abuf[branch, y, j],
+                    wo[y, pl.ds(j * GROUP, GROUP), :],
+                    preferred_element_type=jnp.float32,
+                )
+                total = part if total is None else total + part
+            acc[branch] += total
+            return carry
+
+        lax.fori_loop(0, NY, one, 0)
+
+    attention_round(0)
+    attention_round(1)
+    gather(0)
+    attention_round(2)
+    gather(1)
+    spread(0)
+    acc[...] = jnp.zeros_like(acc)
+    wo_own.wait()
+    for dy in (1, 2, 3):
+        w_copy(dy).wait_recv()
+    gather(2)
+    spread(1)
+    for j in (0, 1):
+        for dy in (0, 1, 2, 3):
+            c_copy(j, dy).wait_recv()
+    for branch in (0, 1):
+        product_of(branch, (0, 1))
+    spread(2)
+    product_of(guid, (2,))
+    for dy in (0, 1, 2, 3):
+        c_copy(2, dy).wait_recv()
+    product_of(1 - guid, (2,))
+
+    for which in (0, 1):
+        p_copy(which).wait_recv()
+    column = pl.ds(pl.multiple_of((guid * NY + tp) * TOK, TILE), TOK)
+    strength = guidance_ref[0]
+    gate_own = mod_ref[2, :, column]
+    gate_other = modother[2, :, column]
+    own = xbuf[:, column].astype(jnp.float32) + gate_own * acc[guid]
+    other = xother[...].astype(jnp.float32) + gate_other * acc[1 - guid]
+    cond = jnp.where(guid == 0, own, other)
+    uncond = jnp.where(guid == 0, other, own)
+    out_ref[...] = (uncond + strength * (cond - uncond)).astype(jnp.bfloat16)
+
+    for which in (0, 1):
+        p_copy(which).wait_send()
+    for dy in (1, 2, 3):
+        w_copy(dy).wait_send()
     for dz in (1, 2, 3):
         meta_copy(dz).wait_send()
     for j in range(ROUNDS):
+        for dy in (1, 2, 3):
+            y_copy(j, dy).wait_send()
+        for dy in (0, 1, 2, 3):
+            c_copy(j, dy).wait_send()
         for dz in (1, 2, 3):
             z_copy(j, dz).wait_send()
             q_copy(j, dz).wait_send()
@@ -307,16 +451,35 @@
                 x_copy_of(j, dz, side).wait_send()
 
 
-def attention(states, modul, w_query, w_key, w_value, block_ids, block_count):
-    width = states.shape[1]
+def shards(
+    hidden_states, modulation, w_query, w_key, w_value, w_out, block_ids, block_count, guidance
+):
+    width = hidden_states.shape[2]
     bf16 = jnp.bfloat16
     dma = pltpu.SemaphoreType.DMA
     any_spec = pl.BlockSpec(memory_space=pltpu.HBM)
     vmem_spec = pl.BlockSpec(memory_space=pltpu.VMEM)
+    smem_spec = pl.BlockSpec(memory_space=pltpu.SMEM)
+    per_round = pltpu.VMEM((ROUNDS, NZ, OWN_TILES, HD, TILE), bf16)
+    pairs = []
+    for shape in (
+        (ROUNDS, 3),
+        (ROUNDS, 4, 2),
+        (ROUNDS, 3),
+        (ROUNDS, 3),
+        (3,),
+        (3,),
+        (ROUNDS, 3),
+        (ROUNDS, 4),
+        (2,),
+    ):
+        pairs += [dma(shape), dma(shape)]
     return pl.pallas_call(
-        attention_kernel,
-        out_shape=jax.ShapeDtypeStruct((TOK, ROUNDS * GROUP), bf16),
-        in_specs=[any_spec, vmem_spec, any_spec, any_spec, any_spec, vmem_spec, vmem_spec],
+        block_kernel,
+        out_shape=jax.ShapeDtypeStruct((TOK, TOK), bf16),
+        in_specs=[any_spec, vmem_spec]
+        + [any_spec] * 4
+        + [vmem_spec, vmem_spec, smem_spec],
         out_specs=vmem_spec,
         scratch_shapes=[
             pltpu.VMEM((TOK, width), bf16),
@@ -326,76 +489,38 @@
             pltpu.VMEM((3 * SLAB, 2, HD, TILE), bf16),
             pltpu.VMEM((3 * SLAB, 2, HD, TILE), bf16),
             pltpu.VMEM((3 * SLAB, 2, HD, TILE), bf16),
-            pltpu.VMEM((ROUNDS, NZ, OWN_TILES, HD, TILE), bf16),
-            pltpu.VMEM((ROUNDS, NZ, OWN_TILES, HD, TILE), bf16),
-            pltpu.VMEM((ROUNDS, NZ, OWN_TILES, HD, TILE), bf16),
-            pltpu.VMEM((ROUNDS, NZ, OWN_TILES, HD, TILE), bf16),
+            per_round,
+            per_round,
+            per_round,
+            per_round,
             pltpu.VMEM((OWN_TILES, SLOTS // 2, TILE, 2 * TILE), jnp.float32),
+            pltpu.VMEM((NY, ROUNDS * GROUP, TOK), bf16),
+            pltpu.VMEM((2, NY, ROUNDS, TOK, GROUP), bf16),
+            pltpu.VMEM((2, TOK, TOK), jnp.float32),
+            pltpu.VMEM((TOK, TOK), bf16),
+            pltpu.VMEM((3, 1, width), jnp.float32),
             pltpu.VMEM((8, 128), jnp.int32),
             pltpu.VMEM((NZ, 8, 128), jnp.int32),
             pltpu.SMEM((NZ, 8, 128), jnp.int32),
-            dma((10,)),
-            dma((ROUNDS, 3)),
-            dma((ROUNDS, 3)),
-            dma((ROUNDS, 4, 2)),
-            dma((ROUNDS, 4, 2)),
-            dma((ROUNDS, 3)),
-            dma((ROUNDS, 3)),
-            dma((ROUNDS, 3)),
-            dma((ROUNDS, 3)),
-            dma((3,)),
-            dma((3,)),
+            dma((11,)),
+            *pairs,
             dma((4,)),
         ],
         compiler_params=pltpu.CompilerParams(
-            collective_id=0, has_side_effects=True, vmem_limit_bytes=56 * 2**20
+            collective_id=0, has_side_effects=True, vmem_limit_bytes=60 * 2**20
         ),
-        name="attention",
-    )(states, modul, w_query, w_key, w_value, block_ids, block_count)
-
-
-def swapped(value, axis, distance):
-    return lax.ppermute(value, axis, [(i, i ^ 1 << distance) for i in range(lax.axis_size(axis))])
-
-
-def shards(
-    hidden_states, modulation, w_query, w_key, w_value, w_out, block_ids, block_count, guidance
-):
-    states = hidden_states[0]
-    modul = modulation[0]
-    ntok = states.shape[0]
-    attn = attention(
-        states, modul, w_query, w_key, w_value, block_ids, block_count.reshape(1, -1)
+        name="block",
+    )(
+        hidden_states,
+        jnp.transpose(modulation, (1, 0, 2)),
+        w_query,
+        w_key,
+        w_value,
+        w_out,
+        block_ids,
+        block_count.reshape(1, -1),
+        guidance,
     )
-    xf = states.astype(jnp.float32)
-    proj = jnp.dot(attn, w_out, preferred_element_type=jnp.float32)
-    scale_now = guidance[0]
-    branch = lax.axis_index("guid")
-    tp_count = lax.axis_size("tp")
-    tp_here = lax.axis_index("tp")
-    model_width = states.shape[1]
-    half = model_width // (2 * tp_count)
-
-    def regroup(array):
-        count = array.shape[0]
-        return jnp.transpose(array.reshape(count, 2, tp_count, half), (0, 2, 1, 3)).reshape(
-            count, model_width
-        )
-
-    shares = lax.psum_scatter(
-        regroup(proj).astype(jnp.bfloat16), "tp", scatter_dimension=1, tiled=True
-    ).astype(jnp.float32)
-    x_part = lax.dynamic_slice_in_dim(regroup(xf), tp_here * 2 * half, 2 * half, 1)
-    gate_part = lax.dynamic_slice_in_dim(
-        regroup(modul[2][None, :]), tp_here * 2 * half, 2 * half, 1
-    )
-    block = (x_part + gate_part * shares).reshape(ntok, 2, half)
-    own = lax.dynamic_slice_in_dim(block, branch, 1, 1)[:, 0]
-    outgoing = lax.dynamic_slice_in_dim(block, 1 - branch, 1, 1)[:, 0]
-    other = swapped(outgoing.astype(jnp.bfloat16), "guid", 0).astype(outgoing.dtype)
-    cond = jnp.where(branch == 0, own, other)
-    uncond = jnp.where(branch == 0, other, own)
-    return (uncond + scale_now * (cond - uncond)).astype(jnp.bfloat16)
 
 
 def solution(mesh):

time: 121 us -> 80 us (0.66)
  waiting for transfers between devices: 24 us -> 0 us
  Pallas kernels: 55.8 us -> 77.4 us
  local copies, waits for them, and re-layouts: 17.8 us -> 1.71 us
  between operations: 14.1 us -> 0.66 us
  matrix products: 4.48 us -> 0 us
  other arithmetic: 3.77 us -> 0 us
    reduce_scatter x1 -> x0, waiting for transfers between devices: 23.4 us -> none  [shards(): lax.psum_scatter(regroup(proj).astype(jnp.bfloat16), 'tp', scatter_dimens...]
    pallas_call x1, Pallas kernels: 55.8 us -> 77.4 us  [shards(): pl.pallas_call(block_kernel, out_shape=jax.ShapeDtypeStruct((TOK, TOK), b...]
    convert_element_type x4 -> x0, local copies, waits for them, and re-layouts: 9.13 us -> none  [the longest x2 8.19 us: shards(): regroup(proj).astype(jnp.bfloat16)]
    dot_general x1 -> x0, matrix products: 4.48 us -> none  [shards(): proj = jnp.dot(attn, w_out, preferred_element_type=jnp.float32)]
    unnamed x6 -> x1, local copies, waits for them, and re-layouts: 5.47 us -> 1.71 us
    reshape x2 -> x0, local copies, waits for them, and re-layouts: 2.45 us -> none  [regroup(): jnp.transpose(array.reshape(count, 2, tp_count, half), (0, 2, 1, 3))]
    reshape x1 -> x0, other arithmetic: 1.98 us -> none  [regroup(): jnp.transpose(array.reshape(count, 2, tp_count, half), (0, 2, 1, 3))]
    add x1 -> x0, other arithmetic: 1.65 us -> none  [shards(): block = (x_part + gate_part * shares).reshape(ntok, 2, half)]
  transfers between devices with their start and end apart: 2 -> 0, of which waited for: 2 -> 0; matrix products, arithmetic and copies ran while one was open for 6% -> 0% of each run, Pallas kernels for 0% -> 0%
where the time goes in v1:
time: 80 us; the launch traced here: 79.8 us
  Pallas kernels  77.4 us (97%)
  local copies, waits for them, and re-layouts  1.71 us (2%)
    pallas_call x1, Pallas kernels, shards(): pl.pallas_call(block_kernel, out_shape=jax.ShapeDtypeStruct((TOK, TOK), b...  77.4 us
    unnamed x1, local copies, waits for them, and re-layouts  1.71 us

profile of v1, /device:TPU:1, one launch (start us, length us, event | category | flops | bytes accessed | tf_op | source)
XLA Modules:
  0.0 79.8 jit_solution(4318220195667425567)
XLA Ops:
  0.7 77.4 %block.1 = bf16[384,384]{1,0:T(8,128)(2,1)} custom-call(bf16[1,384,3072]{2,1,0:T(8,128)(2,1)} %x_hbm.1, f32[3,1,3072]{2,1,0:T(1,128)} %bitcast.2, bf16[3072,768]{1,0:T(8,128)(2,1)} %wq_hbm.1, bf16[3072,768]{1,0:T(8,128)(2,1)} %wk_hbm.1, bf16[3072,768]{1,0:T(8,128)(2,1)} %wv_hbm.1, bf16[768,3072]{1,0:T(8,128)(2,1)} %wo_hbm.1, s32[3,12]{1,0:T(4,128)} %ids_ref.1, ...), custom_call_target="tpu_custom_call" | custom-call | tf_op jit(solution)/shard_map/block/pallas_call | solution.py:477
  78.1 1.7 %copy.12 = bf16[384,384]{1,0:T(8,128)(2,1)} copy(bf16[384,384]{1,0:T(8,128)(2,1)} %block.1) | data formatting | bytes 589824

commit v2 on v1

--- a/solution.py
+++ b/solution.py
@@ -1,5 +1,4 @@
 import functools
-import math
 
 import jax
 import jax.numpy as jnp
@@ -11,7 +10,6 @@
 HD = 64
 TILE = 128
 MESH = pl.DeviceIdType.MESH
-EXP_SCALE = 0.125 * math.log2(math.e)
 
 NZ = 4
 NY = 4
@@ -73,6 +71,8 @@
     c_recv,
     p_send,
     p_recv,
+    f_send,
+    f_recv,
     local_sem,
 ):
     seq = lax.axis_index("seq")
@@ -202,6 +202,18 @@
             send_sem=y_send.at[j, dy - 1],
             recv_sem=y_recv.at[j, dy - 1],
             device_id=y_peer(dy),
+            device_id_type=MESH,
+        )
+
+    def f_copy(j, way):
+        step = 1 - 2 * way
+        half = abuf.at[guid, (tp - step + NY) % NY, j, pl.ds(way * (TOK // 2), TOK // 2)]
+        return pltpu.make_async_remote_copy(
+            src_ref=half,
+            dst_ref=half,
+            send_sem=f_send.at[j, way],
+            recv_sem=f_recv.at[j, way],
+            device_id=y_peer((step + NY) % NY),
             device_id_type=MESH,
         )
 
@@ -254,7 +266,7 @@
         )
         return carry
 
-    lax.fori_loop(0, TOK // rows, norm_rows, 0)
+    lax.fori_loop(0, TOK // rows, norm_rows, 0, unroll=8)
 
     def product(slot):
         weights[slot].wait()
@@ -308,8 +320,8 @@
     one_rows = jnp.ones((HD, TILE), jnp.bfloat16)
     zero_rows = jnp.zeros((HD, TILE), jnp.bfloat16)
 
-    def attend(j, owner, i):
-        q = jnp.transpose(qbuf[j, owner, i])
+    def attend(j, owner, i, spot_of):
+        q = jnp.transpose(qbuf[j, owner, i]) * jnp.asarray(0.125, jnp.bfloat16)
         top = None
         where = []
         for c in range(0, SLOTS, 2):
@@ -319,13 +331,13 @@
             where.append(spots)
             pair = jnp.concatenate([kv[j][spot, 0] for spot in spots], axis=1)
             s = jnp.dot(q, pair, preferred_element_type=jnp.float32)
-            scores[i, c // 2] = s
+            scores[spot_of, c // 2] = s
             top = s if top is None else jnp.maximum(top, s)
         top = jnp.max(top, axis=1, keepdims=True)
         live = meta_smem[owner, 3, i]
         acc = None
         for c in range(0, SLOTS, 2):
-            p = jnp.exp2((scores[i, c // 2] - top) * EXP_SCALE).astype(jnp.bfloat16)
+            p = jnp.exp(scores[spot_of, c // 2] - top).astype(jnp.bfloat16)
             sides = []
             for e in (0, 1):
                 ok = (c + e) < live
@@ -355,13 +367,10 @@
         for dz in (1, 2, 3):
             q_copy(j, dz).wait_recv()
 
-        def owner_step(step, carry):
+        for step in range(NZ):
             owner = (pz + step + 1) % NZ
             for i in range(OWN_TILES):
-                attend(j, owner, i)
-            return carry
-
-        lax.fori_loop(0, NZ, owner_step, 0)
+                attend(j, owner, i, step * OWN_TILES + i)
         for dz in (1, 2, 3):
             r_copy(j, dz).start()
         back[j, pz] = ret[j, pz]
@@ -372,14 +381,20 @@
         for i in range(OWN_TILES):
             part = back[j, :, i].reshape(GROUP, TILE)
             abuf[guid, tp, j, pl.ds(i * TILE, TILE), :] = jnp.transpose(part)
-        for dy in (1, 3, 2):
+        for dy in (1, 3):
             y_copy(j, dy).start()
         c_copy(j, 0).start()
 
     def spread(j):
-        for dy in (1, 3, 2):
+        for dy in (1, 3):
             y_copy(j, dy).wait_recv()
+            f_copy(j, dy // 2).start()
             c_copy(j, dy).start()
+
+    def spread_far(j):
+        for way in (0, 1):
+            f_copy(j, way).wait_recv()
+        c_copy(j, 2).start()
 
     def product_of(branch, js):
         def one(y, carry):
@@ -396,33 +411,40 @@
 
         lax.fori_loop(0, NY, one, 0)
 
+    def arrived(j):
+        for dy in (0, 1, 2, 3):
+            c_copy(j, dy).wait_recv()
+
+    acc[...] = jnp.zeros_like(acc)
     attention_round(0)
+    gather(0)
     attention_round(1)
-    gather(0)
+    spread(0)
+    gather(1)
     attention_round(2)
-    gather(1)
-    spread(0)
-    acc[...] = jnp.zeros_like(acc)
+    spread_far(0)
+    spread(1)
     wo_own.wait()
     for dy in (1, 2, 3):
         w_copy(dy).wait_recv()
+    arrived(0)
+    for branch in (0, 1):
+        product_of(branch, (0,))
     gather(2)
-    spread(1)
-    for j in (0, 1):
-        for dy in (0, 1, 2, 3):
-            c_copy(j, dy).wait_recv()
+    spread_far(1)
+    arrived(1)
     for branch in (0, 1):
-        product_of(branch, (0, 1))
+        product_of(branch, (1,))
     spread(2)
+    spread_far(2)
     product_of(guid, (2,))
-    for dy in (0, 1, 2, 3):
-        c_copy(2, dy).wait_recv()
+    arrived(2)
     product_of(1 - guid, (2,))
 
     for which in (0, 1):
         p_copy(which).wait_recv()
     column = pl.ds(pl.multiple_of((guid * NY + tp) * TOK, TILE), TOK)
-    strength = guidance_ref[0]
+    strength = guidance_ref[...]
     gate_own = mod_ref[2, :, column]
     gate_other = modother[2, :, column]
     own = xbuf[:, column].astype(jnp.float32) + gate_own * acc[guid]
@@ -438,8 +460,10 @@
     for dz in (1, 2, 3):
         meta_copy(dz).wait_send()
     for j in range(ROUNDS):
-        for dy in (1, 2, 3):
+        for dy in (1, 3):
             y_copy(j, dy).wait_send()
+        for way in (0, 1):
+            f_copy(j, way).wait_send()
         for dy in (0, 1, 2, 3):
             c_copy(j, dy).wait_send()
         for dz in (1, 2, 3):
@@ -459,7 +483,6 @@
     dma = pltpu.SemaphoreType.DMA
     any_spec = pl.BlockSpec(memory_space=pltpu.HBM)
     vmem_spec = pl.BlockSpec(memory_space=pltpu.VMEM)
-    smem_spec = pl.BlockSpec(memory_space=pltpu.SMEM)
     per_round = pltpu.VMEM((ROUNDS, NZ, OWN_TILES, HD, TILE), bf16)
     pairs = []
     for shape in (
@@ -472,6 +495,7 @@
         (ROUNDS, 3),
         (ROUNDS, 4),
         (2,),
+        (ROUNDS, 2),
     ):
         pairs += [dma(shape), dma(shape)]
     return pl.pallas_call(
@@ -479,7 +503,7 @@
         out_shape=jax.ShapeDtypeStruct((TOK, TOK), bf16),
         in_specs=[any_spec, vmem_spec]
         + [any_spec] * 4
-        + [vmem_spec, vmem_spec, smem_spec],
+        + [vmem_spec] * 3,
         out_specs=vmem_spec,
         scratch_shapes=[
             pltpu.VMEM((TOK, width), bf16),
@@ -493,7 +517,7 @@
             per_round,
             per_round,
             per_round,
-            pltpu.VMEM((OWN_TILES, SLOTS // 2, TILE, 2 * TILE), jnp.float32),
+            pltpu.VMEM((SLAB, SLOTS // 2, TILE, 2 * TILE), jnp.float32),
             pltpu.VMEM((NY, ROUNDS * GROUP, TOK), bf16),
             pltpu.VMEM((2, NY, ROUNDS, TOK, GROUP), bf16),
             pltpu.VMEM((2, TOK, TOK), jnp.float32),
@@ -519,7 +543,7 @@
         w_out,
         block_ids,
         block_count.reshape(1, -1),
-        guidance,
+        guidance.reshape(1, 1),
     )
 
 

time: 80 us -> 73.7 us (0.921)
  Pallas kernels: 77.4 us -> 71.2 us
    pallas_call x1, Pallas kernels: 77.4 us -> 71.2 us  [shards(): pl.pallas_call(block_kernel, out_shape=jax.ShapeDtypeStruct((TOK, TOK), b...]
where the time goes in v2:
time: 73.7 us; the launch traced here: 73.5 us
  Pallas kernels  71.2 us (97%)
  local copies, waits for them, and re-layouts  1.71 us (2%)
    pallas_call x1, Pallas kernels, shards(): pl.pallas_call(block_kernel, out_shape=jax.ShapeDtypeStruct((TOK, TOK), b...  71.2 us
    unnamed x1, local copies, waits for them, and re-layouts  1.71 us

profile of v2, /device:TPU:1, one launch (start us, length us, event | category | flops | bytes accessed | tf_op | source)
XLA Modules:
  0.0 73.5 jit_solution(608162196268742441)
XLA Ops:
  0.7 71.2 %block.1 = bf16[384,384]{1,0:T(8,128)(2,1)} custom-call(bf16[1,384,3072]{2,1,0:T(8,128)(2,1)} %x_hbm.1, f32[3,1,3072]{2,1,0:T(1,128)} %bitcast.4, bf16[3072,768]{1,0:T(8,128)(2,1)} %wq_hbm.1, bf16[3072,768]{1,0:T(8,128)(2,1)} %wk_hbm.1, bf16[3072,768]{1,0:T(8,128)(2,1)} %wv_hbm.1, bf16[768,3072]{1,0:T(8,128)(2,1)} %wo_hbm.1, s32[3,12]{1,0:T(4,128)} %ids_ref.1, ...), custom_call_target="tpu_custom_call" | custom-call | tf_op jit(solution)/shard_map/block/pallas_call | solution.py:501
  71.8 1.7 %copy.12 = bf16[384,384]{1,0:T(8,128)(2,1)} copy(bf16[384,384]{1,0:T(8,128)(2,1)} %block.1) | data formatting | bytes 589824

commit v3 on v2

--- a/solution.py
+++ b/solution.py
@@ -19,6 +19,7 @@
 SLOTS = 12
 TOK = OWN_TILES * TILE
 GROUP = NZ * HD
+PIECES = ((0, 0, 3), (1, 0, 3), (2, 0, 1), (2, 1, 1), (2, 2, 1))
 
 
 def block_kernel(
@@ -93,25 +94,27 @@
 
     partner = (seq, 1 - guid, tp)
 
-    x_copy = pltpu.make_async_copy(x_hbm.at[0], xbuf, load_sem.at[9])
-    x_copy.start()
-    weights = {}
-    order = [(kind, j) for j in range(ROUNDS) for kind in (1, 2)] + [(0, j) for j in range(ROUNDS)]
-    for kind, j in order:
+    def x_load(i):
+        rows = pl.ds(i * TILE, TILE)
+        return pltpu.make_async_copy(x_hbm.at[0, rows], xbuf.at[rows], load_sem.at[9 + i])
+
+    def w_load(kind, j):
         source = (wq_hbm, wk_hbm, wv_hbm)[kind]
         slot = kind * ROUNDS + j
-        copy = pltpu.make_async_copy(
+        return pltpu.make_async_copy(
             source.at[:, pl.ds(j * GROUP, GROUP)], wbuf.at[slot], load_sem.at[slot]
         )
-        copy.start()
-        weights[slot] = copy
+
+    for i in range(OWN_TILES):
+        x_load(i).start()
+    w_load(1, 0).start()
+    w_load(2, 0).start()
 
     wo_own = pltpu.make_async_copy(
         wo_hbm.at[:, pl.ds(pl.multiple_of((guid * NY + tp) * TOK, TILE), TOK)],
         wo.at[tp],
-        load_sem.at[10],
+        load_sem.at[12],
     )
-    wo_own.start()
 
     meta[...] = jnp.zeros_like(meta)
     meta[0:3, 0:SLOTS] = ids_ref[...]
@@ -174,12 +177,14 @@
             device_id_type=MESH,
         )
 
-    def r_copy(j, dz):
-        return pltpu.make_async_remote_copy(
-            src_ref=ret.at[j, (pz + dz) % NZ],
-            dst_ref=back.at[j, pz],
-            send_sem=r_send.at[j, dz - 1],
-            recv_sem=r_recv.at[j, dz - 1],
+    def r_copy(p, dz):
+        j, first_tile, count = PIECES[p]
+        tiles = pl.ds(first_tile, count)
+        return pltpu.make_async_remote_copy(
+            src_ref=ret.at[j, (pz + dz) % NZ, tiles],
+            dst_ref=back.at[j, pz, tiles],
+            send_sem=r_send.at[p, dz - 1],
+            recv_sem=r_recv.at[p, dz - 1],
             device_id=z_peer(dz),
             device_id_type=MESH,
         )
@@ -195,35 +200,43 @@
             device_id_type=MESH,
         )
 
-    def y_copy(j, dy):
-        return pltpu.make_async_remote_copy(
-            src_ref=abuf.at[guid, tp, j],
-            dst_ref=abuf.at[guid, tp, j],
-            send_sem=y_send.at[j, dy - 1],
-            recv_sem=y_recv.at[j, dy - 1],
+    def y_copy(p, dy):
+        j, first_tile, count = PIECES[p]
+        part = abuf.at[guid, tp, j, pl.ds(first_tile * TILE, count * TILE)]
+        return pltpu.make_async_remote_copy(
+            src_ref=part,
+            dst_ref=part,
+            send_sem=y_send.at[p, dy // 2],
+            recv_sem=y_recv.at[p, dy // 2],
             device_id=y_peer(dy),
             device_id_type=MESH,
         )
 
-    def f_copy(j, way):
+    def f_copy(p, way):
+        j, first_tile, count = PIECES[p]
         step = 1 - 2 * way
-        half = abuf.at[guid, (tp - step + NY) % NY, j, pl.ds(way * (TOK // 2), TOK // 2)]
+        size = count * TILE // 2
+        half = abuf.at[
+            guid, (tp - step + NY) % NY, j, pl.ds(first_tile * TILE + way * size, size)
+        ]
         return pltpu.make_async_remote_copy(
             src_ref=half,
             dst_ref=half,
-            send_sem=f_send.at[j, way],
-            recv_sem=f_recv.at[j, way],
+            send_sem=f_send.at[p, way],
+            recv_sem=f_recv.at[p, way],
             device_id=y_peer((step + NY) % NY),
             device_id_type=MESH,
         )
 
-    def c_copy(j, dy):
+    def c_copy(p, dy):
+        j, first_tile, count = PIECES[p]
         origin = (tp - dy + NY) % NY
-        return pltpu.make_async_remote_copy(
-            src_ref=abuf.at[guid, origin, j],
-            dst_ref=abuf.at[guid, origin, j],
-            send_sem=c_send.at[j, dy],
-            recv_sem=c_recv.at[j, dy],
+        part = abuf.at[guid, origin, j, pl.ds(first_tile * TILE, count * TILE)]
+        return pltpu.make_async_remote_copy(
+            src_ref=part,
+            dst_ref=part,
+            send_sem=c_send.at[p, dy],
+            recv_sem=c_recv.at[p, dy],
             device_id=partner,
             device_id_type=MESH,
         )
@@ -243,33 +256,34 @@
             device_id_type=MESH,
         )
 
-    for dz in (1, 2, 3):
-        meta_copy(dz).start()
-    for dy in (1, 3, 2):
-        w_copy(dy).start()
-
-    x_copy.wait()
-    for which in (0, 1):
-        p_copy(which).start()
     rows = 16
-
-    def norm_rows(i, carry):
-        at = pl.ds(pl.multiple_of(i * rows, rows), rows)
-        xf = xbuf[at, :].astype(jnp.float32)
-        width = xf.shape[1]
-        mean = jnp.sum(xf, axis=1, keepdims=True) * (1.0 / width)
-        off = xf - mean
-        var = jnp.sum(off * off, axis=1, keepdims=True) * (1.0 / width)
-        scale = 1.0 / jnp.sqrt(var + 1e-05)
-        hbuf[at, :] = (off * scale * (1.0 + mod_ref[1]) + mod_ref[0]).astype(
-            jnp.bfloat16
-        )
-        return carry
-
-    lax.fori_loop(0, TOK // rows, norm_rows, 0, unroll=8)
+    gain = 1.0 + mod_ref[1]
+    for i in range(OWN_TILES):
+        x_load(i).wait()
+        if i == 0:
+            w_load(1, 1).start()
+            w_load(2, 1).start()
+        if i == 1:
+            w_load(1, 2).start()
+            w_load(2, 2).start()
+
+        def norm_rows(n, carry, i=i):
+            at = pl.ds(pl.multiple_of(i * TILE + n * rows, rows), rows)
+            xf = xbuf[at, :].astype(jnp.float32)
+            width = xf.shape[1]
+            mean = jnp.sum(xf, axis=1, keepdims=True) * (1.0 / width)
+            off = xf - mean
+            var = jnp.sum(off * off, axis=1, keepdims=True) * (1.0 / width)
+            scale = 1.0 / jnp.sqrt(var + 1e-05)
+            hbuf[at, :] = (off * scale * gain + mod_ref[0]).astype(jnp.bfloat16)
+            return carry
+
+        lax.fori_loop(0, TILE // rows, norm_rows, 0, unroll=8)
+    for j in range(ROUNDS):
+        w_load(0, j).start()
 
     def product(slot):
-        weights[slot].wait()
+        w_load(slot // ROUNDS, slot % ROUNDS).wait()
         full = jnp.dot(hbuf[...], wbuf[slot], preferred_element_type=jnp.float32)
         return full.astype(jnp.bfloat16)
 
@@ -284,7 +298,7 @@
                 stage[j, :, i, which] = part
 
     def forward(j):
-        for dz in (1, 2, 3):
+        for dz in (1, 3, 2):
             z_copy(j, dz).wait_recv()
             for side in (0, 1):
                 x_copy_of(j, dz, side).start()
@@ -292,23 +306,41 @@
     def make_q(j):
         for i, part in tiles_of(product(j)):
             qstage[j, :, i] = part
-        for dz in (1, 2, 3):
+        qbuf[j, pz] = qstage[j, pz]
+
+    def send_z(j):
+        for dz in (1, 3, 2):
+            z_copy(j, dz).start()
+
+    def send_q(j):
+        for dz in (1, 3, 2):
             q_copy(j, dz).start()
-        qbuf[j, pz] = qstage[j, pz]
 
     for j in range(ROUNDS):
         make_kv(j)
-        for dz in (1, 2, 3):
-            z_copy(j, dz).start()
+        if j == 0:
+            send_z(0)
         for side in (0, 1):
             x_copy_of(j, 0, side).start()
         own_copy(j).start()
+        if j == 0:
+            for dz in (1, 2, 3):
+                meta_copy(dz).start()
+            for which in (0, 1):
+                p_copy(which).start()
+            for dy in (1, 3, 2):
+                w_copy(dy).start()
+    wo_own.start()
+    make_q(0)
     forward(0)
-    make_q(0)
+    send_z(1)
+    send_q(0)
+    make_q(1)
+    make_q(2)
     forward(1)
-    make_q(1)
-    forward(2)
-    make_q(2)
+    send_z(2)
+    send_q(1)
+    send_q(2)
 
     for dz in (1, 2, 3):
         meta_copy(dz).wait_recv()
@@ -359,99 +391,124 @@
         both = jnp.transpose(acc)
         ret[j, owner, i] = (both[:HD] / both[HD:]).astype(jnp.bfloat16)
 
-    def attention_round(j):
+    def ready(j):
         own_copy(j).wait()
-        for dz in (0, 1, 2, 3):
+        for dz in (0, 1, 3, 2):
             for side in (0, 1):
                 x_copy_of(j, dz, side).wait_recv()
-        for dz in (1, 2, 3):
+        for dz in (1, 3, 2):
             q_copy(j, dz).wait_recv()
 
+    def attention_piece(p):
+        j, first_tile, count = PIECES[p]
         for step in range(NZ):
             owner = (pz + step + 1) % NZ
-            for i in range(OWN_TILES):
+            for i in range(first_tile, first_tile + count):
                 attend(j, owner, i, step * OWN_TILES + i)
-        for dz in (1, 2, 3):
-            r_copy(j, dz).start()
-        back[j, pz] = ret[j, pz]
-
-    def gather(j):
-        for dz in (1, 2, 3):
-            r_copy(j, dz).wait_recv()
-        for i in range(OWN_TILES):
+        for dz in (1, 3, 2):
+            r_copy(p, dz).start()
+        tiles = pl.ds(first_tile, count)
+        back[j, pz, tiles] = ret[j, pz, tiles]
+
+    def gather(p):
+        j, first_tile, count = PIECES[p]
+        for dz in (1, 3, 2):
+            r_copy(p, dz).wait_recv()
+        for i in range(first_tile, first_tile + count):
             part = back[j, :, i].reshape(GROUP, TILE)
             abuf[guid, tp, j, pl.ds(i * TILE, TILE), :] = jnp.transpose(part)
         for dy in (1, 3):
-            y_copy(j, dy).start()
-        c_copy(j, 0).start()
-
-    def spread(j):
+            y_copy(p, dy).start()
+        c_copy(p, 0).start()
+
+    def spread(p):
         for dy in (1, 3):
-            y_copy(j, dy).wait_recv()
-            f_copy(j, dy // 2).start()
-            c_copy(j, dy).start()
-
-    def spread_far(j):
+            y_copy(p, dy).wait_recv()
+            f_copy(p, dy // 2).start()
+            c_copy(p, dy).start()
+
+    def spread_far(p):
         for way in (0, 1):
-            f_copy(j, way).wait_recv()
-        c_copy(j, 2).start()
-
-    def product_of(branch, js):
-        def one(y, carry):
-            total = None
-            for j in js:
-                part = jnp.dot(
-                    abuf[branch, y, j],
-                    wo[y, pl.ds(j * GROUP, GROUP), :],
-                    preferred_element_type=jnp.float32,
-                )
-                total = part if total is None else total + part
-            acc[branch] += total
-            return carry
-
-        lax.fori_loop(0, NY, one, 0)
-
-    def arrived(j):
-        for dy in (0, 1, 2, 3):
-            c_copy(j, dy).wait_recv()
+            f_copy(p, way).wait_recv()
+        c_copy(p, 2).start()
+
+    def arrived(p):
+        for dy in (0, 1, 3, 2):
+            c_copy(p, dy).wait_recv()
+
+    def part_of(branch, p, y):
+        j, first_tile, count = PIECES[p]
+        return jnp.dot(
+            abuf[branch, y, j, pl.ds(first_tile * TILE, count * TILE), :],
+            wo[y, pl.ds(j * GROUP, GROUP), :],
+            preferred_element_type=jnp.float32,
+        )
+
+    def accumulate(p):
+        arrived(p)
+        for branch in (0, 1):
+
+            def one(y, carry, branch=branch):
+                acc[branch] += part_of(branch, p, y)
+                return carry
+
+            lax.fori_loop(0, NY, one, 0)
+
+    column = pl.ds(pl.multiple_of((guid * NY + tp) * TOK, TILE), TOK)
+
+    def finish(p):
+        j, first_tile, count = PIECES[p]
+        at = pl.ds(first_tile * TILE, count * TILE)
+        strength = guidance_ref[...]
+
+        def total(branch):
+            summed = acc[branch, at, :]
+            for y in range(NY):
+                summed = summed + part_of(branch, p, y)
+            return summed
+
+        own = xbuf[at, column].astype(jnp.float32) + mod_ref[2, :, column] * total(guid)
+        arrived(p)
+        other = xother[at, :].astype(jnp.float32) + modother[2, :, column] * total(1 - guid)
+        cond = jnp.where(guid == 0, own, other)
+        uncond = jnp.where(guid == 0, other, own)
+        out_ref[at, :] = (uncond + strength * (cond - uncond)).astype(jnp.bfloat16)
 
     acc[...] = jnp.zeros_like(acc)
-    attention_round(0)
+    ready(0)
+    attention_piece(0)
+    forward(2)
     gather(0)
-    attention_round(1)
+    ready(1)
+    attention_piece(1)
     spread(0)
     gather(1)
-    attention_round(2)
+    ready(2)
+    attention_piece(2)
     spread_far(0)
     spread(1)
+    attention_piece(3)
+    gather(2)
+    spread_far(1)
+    attention_piece(4)
+    gather(3)
+    spread(2)
     wo_own.wait()
     for dy in (1, 2, 3):
         w_copy(dy).wait_recv()
-    arrived(0)
-    for branch in (0, 1):
-        product_of(branch, (0,))
-    gather(2)
-    spread_far(1)
-    arrived(1)
-    for branch in (0, 1):
-        product_of(branch, (1,))
-    spread(2)
+    accumulate(0)
+    gather(4)
+    spread(3)
     spread_far(2)
-    product_of(guid, (2,))
-    arrived(2)
-    product_of(1 - guid, (2,))
-
+    accumulate(1)
+    spread(4)
+    spread_far(3)
     for which in (0, 1):
         p_copy(which).wait_recv()
-    column = pl.ds(pl.multiple_of((guid * NY + tp) * TOK, TILE), TOK)
-    strength = guidance_ref[...]
-    gate_own = mod_ref[2, :, column]
-    gate_other = modother[2, :, column]
-    own = xbuf[:, column].astype(jnp.float32) + gate_own * acc[guid]
-    other = xother[...].astype(jnp.float32) + gate_other * acc[1 - guid]
-    cond = jnp.where(guid == 0, own, other)
-    uncond = jnp.where(guid == 0, other, own)
-    out_ref[...] = (uncond + strength * (cond - uncond)).astype(jnp.bfloat16)
+    finish(2)
+    spread_far(4)
+    finish(3)
+    finish(4)
 
     for which in (0, 1):
         p_copy(which).wait_send()
@@ -460,19 +517,21 @@
     for dz in (1, 2, 3):
         meta_copy(dz).wait_send()
     for j in range(ROUNDS):
-        for dy in (1, 3):
-            y_copy(j, dy).wait_send()
-        for way in (0, 1):
-            f_copy(j, way).wait_send()
-        for dy in (0, 1, 2, 3):
-            c_copy(j, dy).wait_send()
         for dz in (1, 2, 3):
             z_copy(j, dz).wait_send()
             q_copy(j, dz).wait_send()
-            r_copy(j, dz).wait_send()
         for dz in (0, 1, 2, 3):
             for side in (0, 1):
                 x_copy_of(j, dz, side).wait_send()
+    for p in range(len(PIECES)):
+        for dz in (1, 2, 3):
+            r_copy(p, dz).wait_send()
+        for dy in (1, 3):
+            y_copy(p, dy).wait_send()
+        for way in (0, 1):
+            f_copy(p, way).wait_send()
+        for dy in (0, 1, 2, 3):
+            c_copy(p, dy).wait_send()
 
 
 def shards(
@@ -485,17 +544,18 @@
     vmem_spec = pl.BlockSpec(memory_space=pltpu.VMEM)
     per_round = pltpu.VMEM((ROUNDS, NZ, OWN_TILES, HD, TILE), bf16)
     pairs = []
+    count = len(PIECES)
     for shape in (
         (ROUNDS, 3),
         (ROUNDS, 4, 2),
         (ROUNDS, 3),
-        (ROUNDS, 3),
+        (count, 3),
         (3,),
         (3,),
-        (ROUNDS, 3),
-        (ROUNDS, 4),
+        (count, 2),
+        (count, 4),
         (2,),
-        (ROUNDS, 2),
+        (count, 2),
     ):
         pairs += [dma(shape), dma(shape)]
     return pl.pallas_call(
@@ -526,7 +586,7 @@
             pltpu.VMEM((8, 128), jnp.int32),
             pltpu.VMEM((NZ, 8, 128), jnp.int32),
             pltpu.SMEM((NZ, 8, 128), jnp.int32),
-            dma((11,)),
+            dma((13,)),
             *pairs,
             dma((4,)),
         ],

time: 73.7 us -> 75.5 us (1.024)
  Pallas kernels: 71.2 us -> 72.9 us
    pallas_call x1, Pallas kernels: 71.2 us -> 72.9 us  [shards(): pl.pallas_call(block_kernel, out_shape=jax.ShapeDtypeStruct((TOK, TOK), b...]
where the time goes in v3:
time: 75.5 us; the launch traced here: 75.3 us
  Pallas kernels  72.9 us (97%)
  local copies, waits for them, and re-layouts  1.71 us (2%)
    pallas_call x1, Pallas kernels, shards(): pl.pallas_call(block_kernel, out_shape=jax.ShapeDtypeStruct((TOK, TOK), b...  72.9 us
    unnamed x1, local copies, waits for them, and re-layouts  1.71 us

profile of v3, /device:TPU:1, one launch (start us, length us, event | category | flops | bytes accessed | tf_op | source)
XLA Modules:
  0.0 75.3 jit_solution(3423869611304658950)
XLA Ops:
  0.7 72.9 %block.1 = bf16[384,384]{1,0:T(8,128)(2,1)} custom-call(bf16[1,384,3072]{2,1,0:T(8,128)(2,1)} %x_hbm.1, f32[3,1,3072]{2,1,0:T(1,128)} %bitcast.4, bf16[3072,768]{1,0:T(8,128)(2,1)} %wq_hbm.1, bf16[3072,768]{1,0:T(8,128)(2,1)} %wk_hbm.1, bf16[3072,768]{1,0:T(8,128)(2,1)} %wv_hbm.1, bf16[768,3072]{1,0:T(8,128)(2,1)} %wo_hbm.1, s32[3,12]{1,0:T(4,128)} %ids_ref.1, ...), custom_call_target="tpu_custom_call" | custom-call | tf_op jit(solution)/shard_map/block/pallas_call | solution.py:561
  73.6 1.7 %copy.12 = bf16[384,384]{1,0:T(8,128)(2,1)} copy(bf16[384,384]{1,0:T(8,128)(2,1)} %block.1) | data formatting | bytes 589824

commit v4 on v3

--- a/solution.py
+++ b/solution.py
@@ -141,7 +141,7 @@
     def z_copy(j, dz):
         return pltpu.make_async_remote_copy(
             src_ref=stage.at[j, (pz + dz) % NZ],
-            dst_ref=kv[j].at[pl.ds(SLAB + pz * OWN_TILES, OWN_TILES)],
+            dst_ref=kv[j].at[pl.ds(SLAB + (NZ - dz) * OWN_TILES, OWN_TILES)],
             send_sem=z_send.at[j, dz - 1],
             recv_sem=z_recv.at[j, dz - 1],
             device_id=z_peer(dz),
@@ -150,19 +150,16 @@
 
     def own_copy(j):
         return pltpu.make_async_copy(
-            stage.at[j, pz],
-            kv[j].at[pl.ds(SLAB + pz * OWN_TILES, OWN_TILES)],
-            local_sem.at[j],
-        )
-
-    def x_copy_of(j, dz, side):
-        origin = (pz - dz + NZ) % NZ
-        here = kv[j].at[pl.ds(SLAB + origin * OWN_TILES, OWN_TILES)]
-        return pltpu.make_async_remote_copy(
-            src_ref=stage.at[j, pz] if dz == 0 else here,
-            dst_ref=kv[j].at[pl.ds(2 * SLAB * side + origin * OWN_TILES, OWN_TILES)],
-            send_sem=x_send.at[j, dz, side],
-            recv_sem=x_recv.at[j, dz, side],
+            stage.at[j, pz], kv[j].at[pl.ds(SLAB, OWN_TILES)], local_sem.at[j]
+        )
+
+    def x_copy_of(j, rest, side):
+        first_slot, count = (OWN_TILES, SLAB - OWN_TILES) if rest else (0, OWN_TILES)
+        return pltpu.make_async_remote_copy(
+            src_ref=kv[j].at[pl.ds(SLAB + first_slot, count)] if rest else stage.at[j, pz],
+            dst_ref=kv[j].at[pl.ds(2 * SLAB * side + first_slot, count)],
+            send_sem=x_send.at[j, rest, side],
+            recv_sem=x_recv.at[j, rest, side],
             device_id=x_peer(1 - 2 * side),
             device_id_type=MESH,
         )
@@ -206,8 +203,8 @@
         return pltpu.make_async_remote_copy(
             src_ref=part,
             dst_ref=part,
-            send_sem=y_send.at[p, dy // 2],
-            recv_sem=y_recv.at[p, dy // 2],
+            send_sem=y_send.at[p, dy - 1],
+            recv_sem=y_recv.at[p, dy - 1],
             device_id=y_peer(dy),
             device_id_type=MESH,
         )
@@ -297,11 +294,13 @@
             for i, part in tiles_of(product((1 + which) * ROUNDS + j)):
                 stage[j, :, i, which] = part
 
-    def forward(j):
+    def z_arrived(j):
         for dz in (1, 3, 2):
             z_copy(j, dz).wait_recv()
-            for side in (0, 1):
-                x_copy_of(j, dz, side).start()
+
+    def forward(j):
+        for side in (0, 1):
+            x_copy_of(j, 1, side).start()
 
     def make_q(j):
         for i, part in tiles_of(product(j)):
@@ -332,23 +331,31 @@
                 w_copy(dy).start()
     wo_own.start()
     make_q(0)
-    forward(0)
+    z_arrived(0)
     send_z(1)
     send_q(0)
+    forward(0)
     make_q(1)
     make_q(2)
-    forward(1)
+    z_arrived(1)
     send_z(2)
     send_q(1)
     send_q(2)
+    forward(1)
 
     for dz in (1, 2, 3):
         meta_copy(dz).wait_recv()
+    listed = meta_all[...]
+    block = (listed * 171) >> 9
+    slab = jnp.clip((block >> 2) - px + 1, 0, 2)
+    slot = slab * SLAB + ((block - pz) & 3) * OWN_TILES + (listed - 3 * block)
+    slot = jnp.clip(slot, 0, 3 * SLAB - 1)
+    row = lax.broadcasted_iota(jnp.int32, listed.shape, 1)
+    meta_all[...] = jnp.where(row == 3, listed, slot)
     meta_load = pltpu.make_async_copy(meta_all, meta_smem, local_sem.at[3])
     meta_load.start()
     meta_load.wait()
 
-    first = (px - 1) * SLAB
     one_rows = jnp.ones((HD, TILE), jnp.bfloat16)
     zero_rows = jnp.zeros((HD, TILE), jnp.bfloat16)
 
@@ -357,9 +364,7 @@
         top = None
         where = []
         for c in range(0, SLOTS, 2):
-            spots = [
-                jnp.clip(meta_smem[owner, i, c + e] - first, 0, 3 * SLAB - 1) for e in (0, 1)
-            ]
+            spots = [meta_smem[owner, i, c + e] for e in (0, 1)]
             where.append(spots)
             pair = jnp.concatenate([kv[j][spot, 0] for spot in spots], axis=1)
             s = jnp.dot(q, pair, preferred_element_type=jnp.float32)
@@ -393,9 +398,9 @@
 
     def ready(j):
         own_copy(j).wait()
-        for dz in (0, 1, 3, 2):
+        for rest in (0, 1):
             for side in (0, 1):
-                x_copy_of(j, dz, side).wait_recv()
+                x_copy_of(j, rest, side).wait_recv()
         for dz in (1, 3, 2):
             q_copy(j, dz).wait_recv()
 
@@ -410,6 +415,9 @@
         tiles = pl.ds(first_tile, count)
         back[j, pz, tiles] = ret[j, pz, tiles]
 
+    def direct(p):
+        return PIECES[p][0] == ROUNDS - 1
+
     def gather(p):
         j, first_tile, count = PIECES[p]
         for dz in (1, 3, 2):
@@ -417,19 +425,23 @@
         for i in range(first_tile, first_tile + count):
             part = back[j, :, i].reshape(GROUP, TILE)
             abuf[guid, tp, j, pl.ds(i * TILE, TILE), :] = jnp.transpose(part)
-        for dy in (1, 3):
+        for dy in (1, 3, 2) if direct(p) else (1, 3):
             y_copy(p, dy).start()
         c_copy(p, 0).start()
 
     def spread(p):
         for dy in (1, 3):
             y_copy(p, dy).wait_recv()
-            f_copy(p, dy // 2).start()
+            if not direct(p):
+                f_copy(p, dy // 2).start()
             c_copy(p, dy).start()
 
     def spread_far(p):
-        for way in (0, 1):
-            f_copy(p, way).wait_recv()
+        if direct(p):
+            y_copy(p, 2).wait_recv()
+        else:
+            for way in (0, 1):
+                f_copy(p, way).wait_recv()
         c_copy(p, 2).start()
 
     def arrived(p):
@@ -474,15 +486,41 @@
         uncond = jnp.where(guid == 0, other, own)
         out_ref[at, :] = (uncond + strength * (cond - uncond)).astype(jnp.bfloat16)
 
+    def sent_kv(j):
+        for dz in (1, 2, 3):
+            z_copy(j, dz).wait_send()
+            q_copy(j, dz).wait_send()
+        for rest in (0, 1):
+            for side in (0, 1):
+                x_copy_of(j, rest, side).wait_send()
+
+    def sent_piece(p):
+        for dz in (1, 2, 3):
+            r_copy(p, dz).wait_send()
+        for dy in (1, 3, 2) if direct(p) else (1, 3):
+            y_copy(p, dy).wait_send()
+        if not direct(p):
+            for way in (0, 1):
+                f_copy(p, way).wait_send()
+        for dy in (0, 1, 2, 3):
+            c_copy(p, dy).wait_send()
+
     acc[...] = jnp.zeros_like(acc)
     ready(0)
     attention_piece(0)
+    z_arrived(2)
     forward(2)
     gather(0)
     ready(1)
     attention_piece(1)
     spread(0)
     gather(1)
+    for which in (0, 1):
+        p_copy(which).wait_recv()
+        p_copy(which).wait_send()
+    for dz in (1, 2, 3):
+        meta_copy(dz).wait_send()
+    sent_kv(0)
     ready(2)
     attention_piece(2)
     spread_far(0)
@@ -492,46 +530,29 @@
     spread_far(1)
     attention_piece(4)
     gather(3)
-    spread(2)
     wo_own.wait()
     for dy in (1, 2, 3):
         w_copy(dy).wait_recv()
     accumulate(0)
     gather(4)
-    spread(3)
+    spread(2)
     spread_far(2)
     accumulate(1)
+    spread(3)
+    spread_far(3)
+    finish(2)
     spread(4)
-    spread_far(3)
-    for which in (0, 1):
-        p_copy(which).wait_recv()
-    finish(2)
     spread_far(4)
+    sent_kv(1)
+    sent_kv(2)
+    for dy in (1, 2, 3):
+        w_copy(dy).wait_send()
+    sent_piece(0)
+    sent_piece(1)
     finish(3)
     finish(4)
-
-    for which in (0, 1):
-        p_copy(which).wait_send()
-    for dy in (1, 2, 3):
-        w_copy(dy).wait_send()
-    for dz in (1, 2, 3):
-        meta_copy(dz).wait_send()
-    for j in range(ROUNDS):
-        for dz in (1, 2, 3):
-            z_copy(j, dz).wait_send()
-            q_copy(j, dz).wait_send()
-        for dz in (0, 1, 2, 3):
-            for side in (0, 1):
-                x_copy_of(j, dz, side).wait_send()
-    for p in range(len(PIECES)):
-        for dz in (1, 2, 3):
-            r_copy(p, dz).wait_send()
-        for dy in (1, 3):
-            y_copy(p, dy).wait_send()
-        for way in (0, 1):
-            f_copy(p, way).wait_send()
-        for dy in (0, 1, 2, 3):
-            c_copy(p, dy).wait_send()
+    for p in (2, 3, 4):
+        sent_piece(p)
 
 
 def shards(
@@ -547,12 +568,12 @@
     count = len(PIECES)
     for shape in (
         (ROUNDS, 3),
-        (ROUNDS, 4, 2),
+        (ROUNDS, 2, 2),
         (ROUNDS, 3),
         (count, 3),
         (3,),
         (3,),
-        (count, 2),
+        (count, 3),
         (count, 4),
         (2,),
         (count, 2),

time: 75.5 us -> 74.4 us (0.985)
  Pallas kernels: 72.9 us -> 71.8 us
    pallas_call x1, Pallas kernels: 72.9 us -> 71.8 us  [shards(): pl.pallas_call(block_kernel, out_shape=jax.ShapeDtypeStruct((TOK, TOK), b...]
where the time goes in v4:
time: 74.4 us; the launch traced here: 74.2 us
  Pallas kernels  71.8 us (97%)
  local copies, waits for them, and re-layouts  1.71 us (2%)
    pallas_call x1, Pallas kernels, shards(): pl.pallas_call(block_kernel, out_shape=jax.ShapeDtypeStruct((TOK, TOK), b...  71.8 us
    unnamed x1, local copies, waits for them, and re-layouts  1.71 us

profile of v4, /device:TPU:1, one launch (start us, length us, event | category | flops | bytes accessed | tf_op | source)
XLA Modules:
  0.0 74.2 jit_solution(10477518330388325325)
XLA Ops:
  0.7 71.8 %block.1 = bf16[384,384]{1,0:T(8,128)(2,1)} custom-call(bf16[1,384,3072]{2,1,0:T(8,128)(2,1)} %x_hbm.1, f32[3,1,3072]{2,1,0:T(1,128)} %bitcast.4, bf16[3072,768]{1,0:T(8,128)(2,1)} %wq_hbm.1, bf16[3072,768]{1,0:T(8,128)(2,1)} %wk_hbm.1, bf16[3072,768]{1,0:T(8,128)(2,1)} %wv_hbm.1, bf16[768,3072]{1,0:T(8,128)(2,1)} %wo_hbm.1, s32[3,12]{1,0:T(4,128)} %ids_ref.1, ...), custom_call_target="tpu_custom_call" | custom-call | tf_op jit(solution)/shard_map/block/pallas_call | solution.py:582
  72.5 1.7 %copy.12 = bf16[384,384]{1,0:T(8,128)(2,1)} copy(bf16[384,384]{1,0:T(8,128)(2,1)} %block.1) | data formatting | bytes 589824

commit v5 on v4

--- a/solution.py
+++ b/solution.py
@@ -342,6 +342,8 @@
     send_q(1)
     send_q(2)
     forward(1)
+    z_arrived(2)
+    forward(2)
 
     for dz in (1, 2, 3):
         meta_copy(dz).wait_recv()
@@ -508,13 +510,9 @@
     acc[...] = jnp.zeros_like(acc)
     ready(0)
     attention_piece(0)
-    z_arrived(2)
-    forward(2)
     gather(0)
     ready(1)
     attention_piece(1)
-    spread(0)
-    gather(1)
     for which in (0, 1):
         p_copy(which).wait_recv()
         p_copy(which).wait_send()
@@ -523,26 +521,27 @@
     sent_kv(0)
     ready(2)
     attention_piece(2)
-    spread_far(0)
-    spread(1)
+    spread(0)
+    gather(1)
     attention_piece(3)
     gather(2)
-    spread_far(1)
     attention_piece(4)
+    spread_far(0)
     gather(3)
+    spread(1)
     wo_own.wait()
     for dy in (1, 2, 3):
         w_copy(dy).wait_recv()
     accumulate(0)
     gather(4)
+    spread_far(1)
     spread(2)
-    spread_far(2)
     accumulate(1)
     spread(3)
-    spread_far(3)
+    spread_far(2)
     finish(2)
     spread(4)
-    spread_far(4)
+    spread_far(3)
     sent_kv(1)
     sent_kv(2)
     for dy in (1, 2, 3):
@@ -550,6 +549,7 @@
     sent_piece(0)
     sent_piece(1)
     finish(3)
+    spread_far(4)
     finish(4)
     for p in (2, 3, 4):
         sent_piece(p)

time: 74.4 us -> 77.5 us (1.042)
  Pallas kernels: 71.8 us -> 74.9 us
    pallas_call x1, Pallas kernels: 71.8 us -> 74.9 us  [shards(): pl.pallas_call(block_kernel, out_shape=jax.ShapeDtypeStruct((TOK, TOK), b...]
where the time goes in v5:
time: 77.5 us; the launch traced here: 77.3 us
  Pallas kernels  74.9 us (97%)
  local copies, waits for them, and re-layouts  1.71 us (2%)
    pallas_call x1, Pallas kernels, shards(): pl.pallas_call(block_kernel, out_shape=jax.ShapeDtypeStruct((TOK, TOK), b...  74.9 us
    unnamed x1, local copies, waits for them, and re-layouts  1.71 us

profile of v5, /device:TPU:1, one launch (start us, length us, event | category | flops | bytes accessed | tf_op | source)
XLA Modules:
  0.0 77.3 jit_solution(2734015735266348561)
XLA Ops:
  0.7 74.9 %block.1 = bf16[384,384]{1,0:T(8,128)(2,1)} custom-call(bf16[1,384,3072]{2,1,0:T(8,128)(2,1)} %x_hbm.1, f32[3,1,3072]{2,1,0:T(1,128)} %bitcast.4, bf16[3072,768]{1,0:T(8,128)(2,1)} %wq_hbm.1, bf16[3072,768]{1,0:T(8,128)(2,1)} %wk_hbm.1, bf16[3072,768]{1,0:T(8,128)(2,1)} %wv_hbm.1, bf16[768,3072]{1,0:T(8,128)(2,1)} %wo_hbm.1, s32[3,12]{1,0:T(4,128)} %ids_ref.1, ...), custom_call_target="tpu_custom_call" | custom-call | tf_op jit(solution)/shard_map/block/pallas_call | solution.py:582
  75.6 1.7 %copy.12 = bf16[384,384]{1,0:T(8,128)(2,1)} copy(bf16[384,384]{1,0:T(8,128)(2,1)} %block.1) | data formatting | bytes 589824

commit v6 on v5

--- a/solution.py
+++ b/solution.py
@@ -253,6 +253,9 @@
             device_id_type=MESH,
         )
 
+    for dy in (1, 3, 2):
+        w_copy(dy).start()
+
     rows = 16
     gain = 1.0 + mod_ref[1]
     for i in range(OWN_TILES):
@@ -315,20 +318,23 @@
         for dz in (1, 3, 2):
             q_copy(j, dz).start()
 
-    for j in range(ROUNDS):
-        make_kv(j)
-        if j == 0:
-            send_z(0)
+    def send_own(j):
         for side in (0, 1):
             x_copy_of(j, 0, side).start()
-        own_copy(j).start()
-        if j == 0:
-            for dz in (1, 2, 3):
-                meta_copy(dz).start()
-            for which in (0, 1):
-                p_copy(which).start()
-            for dy in (1, 3, 2):
-                w_copy(dy).start()
+
+    make_kv(0)
+    send_z(0)
+    send_own(0)
+    own_copy(0).start()
+    for dz in (1, 2, 3):
+        meta_copy(dz).start()
+    for which in (0, 1):
+        p_copy(which).start()
+    make_kv(1)
+    send_own(1)
+    own_copy(1).start()
+    make_kv(2)
+    own_copy(2).start()
     wo_own.start()
     make_q(0)
     z_arrived(0)
@@ -337,14 +343,6 @@
     forward(0)
     make_q(1)
     make_q(2)
-    z_arrived(1)
-    send_z(2)
-    send_q(1)
-    send_q(2)
-    forward(1)
-    z_arrived(2)
-    forward(2)
-
     for dz in (1, 2, 3):
         meta_copy(dz).wait_recv()
     listed = meta_all[...]
@@ -508,10 +506,18 @@
             c_copy(p, dy).wait_send()
 
     acc[...] = jnp.zeros_like(acc)
+    z_arrived(1)
+    send_z(2)
+    send_q(1)
     ready(0)
+    forward(1)
     attention_piece(0)
+    z_arrived(2)
+    send_q(2)
+    ready(1)
+    send_own(2)
+    forward(2)
     gather(0)
-    ready(1)
     attention_piece(1)
     for which in (0, 1):
         p_copy(which).wait_recv()
@@ -519,14 +525,14 @@
     for dz in (1, 2, 3):
         meta_copy(dz).wait_send()
     sent_kv(0)
+    spread(0)
+    gather(1)
     ready(2)
     attention_piece(2)
-    spread(0)
-    gather(1)
+    spread_far(0)
     attention_piece(3)
     gather(2)
     attention_piece(4)
-    spread_far(0)
     gather(3)
     spread(1)
     wo_own.wait()

time: 77.5 us -> 73.7 us (0.951)
  Pallas kernels: 74.9 us -> 71.1 us
    pallas_call x1, Pallas kernels: 74.9 us -> 71.1 us  [shards(): pl.pallas_call(block_kernel, out_shape=jax.ShapeDtypeStruct((TOK, TOK), b...]
where the time goes in v6:
time: 73.7 us; the launch traced here: 73.5 us
  Pallas kernels  71.1 us (96%)
  local copies, waits for them, and re-layouts  1.71 us (2%)
    pallas_call x1, Pallas kernels, shards(): pl.pallas_call(block_kernel, out_shape=jax.ShapeDtypeStruct((TOK, TOK), b...  71.1 us
    unnamed x1, local copies, waits for them, and re-layouts  1.71 us

profile of v6, /device:TPU:1, one launch (start us, length us, event | category | flops | bytes accessed | tf_op | source)
XLA Modules:
  0.0 73.5 jit_solution(10766383910403906006)
XLA Ops:
  0.7 71.1 %block.1 = bf16[384,384]{1,0:T(8,128)(2,1)} custom-call(bf16[1,384,3072]{2,1,0:T(8,128)(2,1)} %x_hbm.1, f32[3,1,3072]{2,1,0:T(1,128)} %bitcast.4, bf16[3072,768]{1,0:T(8,128)(2,1)} %wq_hbm.1, bf16[3072,768]{1,0:T(8,128)(2,1)} %wk_hbm.1, bf16[3072,768]{1,0:T(8,128)(2,1)} %wv_hbm.1, bf16[768,3072]{1,0:T(8,128)(2,1)} %wo_hbm.1, s32[3,12]{1,0:T(4,128)} %ids_ref.1, ...), custom_call_target="tpu_custom_call" | custom-call | tf_op jit(solution)/shard_map/block/pallas_call | solution.py:588
  71.7 1.7 %copy.12 = bf16[384,384]{1,0:T(8,128)(2,1)} copy(bf16[384,384]{1,0:T(8,128)(2,1)} %block.1) | data formatting | bytes 589824

commit v7 on v6

--- a/solution.py
+++ b/solution.py
@@ -525,21 +525,21 @@
     for dz in (1, 2, 3):
         meta_copy(dz).wait_send()
     sent_kv(0)
-    spread(0)
-    gather(1)
     ready(2)
     attention_piece(2)
-    spread_far(0)
+    gather(1)
+    spread(0)
     attention_piece(3)
     gather(2)
     attention_piece(4)
+    spread_far(0)
     gather(3)
+    gather(4)
     spread(1)
     wo_own.wait()
     for dy in (1, 2, 3):
         w_copy(dy).wait_recv()
     accumulate(0)
-    gather(4)
     spread_far(1)
     spread(2)
     accumulate(1)

time: 73.7 us -> 76.1 us (1.033)
  Pallas kernels: 71.1 us -> 73.5 us
    pallas_call x1, Pallas kernels: 71.1 us -> 73.5 us  [shards(): pl.pallas_call(block_kernel, out_shape=jax.ShapeDtypeStruct((TOK, TOK), b...]
where the time goes in v7:
time: 76.1 us; the launch traced here: 75.9 us
  Pallas kernels  73.5 us (97%)
  local copies, waits for them, and re-layouts  1.71 us (2%)
    pallas_call x1, Pallas kernels, shards(): pl.pallas_call(block_kernel, out_shape=jax.ShapeDtypeStruct((TOK, TOK), b...  73.5 us
    unnamed x1, local copies, waits for them, and re-layouts  1.71 us

profile of v7, /device:TPU:1, one launch (start us, length us, event | category | flops | bytes accessed | tf_op | source)
XLA Modules:
  0.0 75.9 jit_solution(9458753832056089682)
XLA Ops:
  0.7 73.5 %block.1 = bf16[384,384]{1,0:T(8,128)(2,1)} custom-call(bf16[1,384,3072]{2,1,0:T(8,128)(2,1)} %x_hbm.1, f32[3,1,3072]{2,1,0:T(1,128)} %bitcast.4, bf16[3072,768]{1,0:T(8,128)(2,1)} %wq_hbm.1, bf16[3072,768]{1,0:T(8,128)(2,1)} %wk_hbm.1, bf16[3072,768]{1,0:T(8,128)(2,1)} %wv_hbm.1, bf16[768,3072]{1,0:T(8,128)(2,1)} %wo_hbm.1, s32[3,12]{1,0:T(4,128)} %ids_ref.1, ...), custom_call_target="tpu_custom_call" | custom-call | tf_op jit(solution)/shard_map/block/pallas_call | solution.py:588
  74.2 1.7 %copy.12 = bf16[384,384]{1,0:T(8,128)(2,1)} copy(bf16[384,384]{1,0:T(8,128)(2,1)} %block.1) | data formatting | bytes 589824
